TPU v7x, 128 devices: a whole 4x4x4 slice. The times are simulated.
128 devices in a mesh: lat: 16 (over y, z), lon: 8 (over x, core).
Axes of the slice: x: 4, y: 4, z: 4, core: 2. Of those that a mesh axis runs over, the one named last changes fastest.
Arguments:
- inputs: bfloat16 [640, 1440, 256], P('lat', 'lon'), may hold values from -6 to 6
- w_enc: bfloat16 [3, 3, 256, 256], replicated, may hold values from -0.125 to 0.125
- w_proj: bfloat16 [256, 128], replicated, may hold values from -0.375 to 0.375
- film_scale: float32 [720, 128], replicated, may hold values from -3 to 3
- film_shift: float32 [720, 128], replicated, may hold values from -3 to 3
- lead_ids: int32 [16], replicated, may hold values from 0 to 719
- w_head: bfloat16 [3, 3, 128, 128], replicated, may hold values from -0.1875 to 0.1875
- zonal_mix: bfloat16 [720, 720], replicated, may hold values from -0.21875 to 0.21875
Outputs:
- forecast: bfloat16 [16, 320, 720, 128], P('lon', 'lat')
Inputs may be any that keep to these rules, and one draw needn't show every extreme that they name: `lead_ids`: rows of the tables; repeats may occur.
All inputs are finite; a program needn't handle non-finite values.
Results may differ from a plain program's by a relative error of at most 0.015.
Values may be sent and summed in bfloat16 or wider, within the bound.
A program may use at most 128 MiB of HBM per device.

v0:
```python
import jax
import jax.numpy as jnp
from jax import lax
from jax.sharding import PartitionSpec as P

LEAD_DEV = 2


def extended(x, sides, width, wrap):
    for axis, dim in sides:
        devices, length = (lax.axis_size(axis), x.shape[dim])
        up = [(i, (i + 1) % devices) for i in range(devices if wrap else devices - 1)]
        down = [(j, i) for i, j in up]
        last = lax.slice_in_dim(x, length - width, length, axis=dim)
        initial = lax.slice_in_dim(x, 0, width, axis=dim)
        before = lax.ppermute(last, axis, up)
        after = lax.ppermute(initial, axis, down)
        x = jnp.concatenate([before, x, after], axis=dim)
    return x


def conv_three(padded, weight):
    batched = padded if padded.ndim == 4 else padded[None]
    result = lax.conv_general_dilated(
        batched,
        weight,
        (1, 1),
        "VALID",
        dimension_numbers=("NHWC", "HWIO", "NHWC"),
        preferred_element_type=jnp.float32,
    )
    return result if padded.ndim == 4 else result[0]


def pool_pairs(field):
    summed = lax.reduce_window(
        field, jnp.array(0, field.dtype), lax.add, (2, 2, 1), (2, 2, 1), "VALID"
    )
    return summed * 0.25


def wrap_columns(field):
    return jnp.concatenate([field[..., -1:, :], field, field[..., :1, :]], axis=-2)


def modulate(projected, scales, shifts):
    widened = projected.astype(jnp.float32)[None]
    return (widened * (1.0 + scales[:, None, None, :]) + shifts[:, None, None, :]).astype(
        jnp.bfloat16
    )


def shards(inputs, w_enc, w_proj, film_scale, film_shift, lead_ids, w_head, zonal_mix):
    lat_rows, lon_cols, channels = inputs.shape
    with_rows = extended(inputs, (("lat", 0),), 1, False)
    padded = extended(with_rows, (("lon", 1),), 1, True)
    encoded = jax.nn.gelu(conv_three(padded, w_enc))
    pooled = pool_pairs(encoded).astype(jnp.bfloat16)
    head_width = w_proj.shape[1]
    lon_group = lax.axis_index("lon")
    my_rows = lax.dynamic_slice_in_dim(lead_ids, lon_group * LEAD_DEV, LEAD_DEV)
    flat = jnp.dot(pooled.reshape(-1, channels), w_proj, preferred_element_type=jnp.float32)
    band_proj = lax.all_gather(
        flat.astype(jnp.bfloat16).reshape(pooled.shape[0], pooled.shape[1], head_width),
        "lon",
        axis=1,
        tiled=True,
    )
    onehot = (my_rows[:, None] == jnp.arange(film_scale.shape[0], dtype=jnp.int32)[None, :]).astype(
        jnp.float32
    )
    scales = jnp.dot(onehot, film_scale, precision=lax.Precision.HIGHEST)
    shifts = jnp.dot(onehot, film_shift, precision=lax.Precision.HIGHEST)
    scales, shifts = (scales, shifts)
    with_band = None
    modulated = modulate(band_proj, scales, shifts)
    with_band = extended(modulated, (("lat", 1),), 1, False)
    padded_head = wrap_columns(with_band)
    hidden = jax.nn.gelu(conv_three(padded_head, w_head)).astype(jnp.bfloat16)
    mixed = jnp.einsum("ij,bajc->baic", zonal_mix, hidden, preferred_element_type=jnp.float32)
    return (modulated.astype(jnp.float32) + mixed).astype(jnp.bfloat16)


def solution(mesh):
    in_specs = (P("lat", "lon", None), P(), P(), P(), P(), P(), P(), P())
    out_specs = P("lon", "lat", None, None)
    return jax.shard_map(shards, mesh=mesh, in_specs=in_specs, out_specs=out_specs, check_vma=False)
```

profile of v0, /device:TPU:96, one launch (start us, length us, event | category | flops | bytes accessed | tf_op | source)
XLA Modules:
  0.0 219.7 jit_solution(3243540371353144879)
XLA Ops:
  6.5 1.8 fusion.43
  8.4 2.4 %collective-permute-start.1 = (bf16[1,180,256]{2,1,0:T(8,128)(2,1)S(1)}, bf16[1,180,256]{2,1,0:T(8,128)(2,1)S(1)}, u32[]{:S(2)}, u32[]{:S(2)}) collective-permute-start(bf16[1,180,256]{2,1,0:T(8,128)(2,1)S(1)} %copy.64), channel_id=1, source_target_pairs={{8,0},{16,8},{24,16},{32,24},{40,32},{48,40},{56,48},{64,56},{72,6... | collective-permute-start | bytes 276488 | tf_op jit(solution)/shard_map/ppermute | solution.py:17
  10.8 5.6 %collective-permute-start = (bf16[1,180,256]{2,1,0:T(8,128)(2,1)S(1)}, bf16[1,180,256]{2,1,0:T(8,128)(2,1)S(1)}, u32[]{:S(2)}, u32[]{:S(2)}) collective-permute-start(bf16[1,180,256]{2,1,0:T(8,128)(2,1)S(1)} %copy.63), channel_id=1, source_target_pairs={{0,8},{8,16},{16,24},{24,32},{32,40},{40,48},{48,56},{56,64},{64,7... | collective-permute-start | bytes 276488 | tf_op jit(solution)/shard_map/ppermute | solution.py:16
  19.6 2.9 %collective-permute-start.3 = (bf16[42,1,256]{2,0,1:T(8,128)(2,1)S(1)}, bf16[42,1,256]{2,0,1:T(8,128)(2,1)S(1)}, u32[]{:S(2)}, u32[]{:S(2)}) collective-permute-start(bf16[42,1,256]{2,0,1:T(8,128)(2,1)S(1)} %get-tuple-element.8), channel_id=1, source_target_pairs={{1,0},{2,1},{3,2},{4,3},{5,4},{6,5},{7,6},{0,7},{9,8},{10,9},{11,1... | collective-permute-start | bytes 64520 | tf_op jit(solution)/shard_map/ppermute | solution.py:17
  24.0 3.2 %maximum_bitcast_fusion = bf16[42,1,182,256]{3,0,2,1:T(8,128)(2,1)S(1)} fusion(bf16[42,1,256]{2,0,1:T(8,128)(2,1)S(1)} %collective-permute-done.3, bf16[1,180,256]{2,0,1:T(2,128)(2,1)S(1)} %copy.46, bf16[40,180,256]{2,0,1:T(8,128)(2,1)S(1)} %copy-done.2, bf16[1,180,256]{2,0,1:T(2,128)(2,1)S(1)} %copy.45, bf16[42,1,256]{2,0,1:T(8,128)(2,1)S(1)} %collective-permute-done.2), kind=kLoop, calls=%fused_computation.37 | loop fusion | flops 19568640 | bytes 7827456 | tf_op jit(solution)/shard_map/broadcast_in_dim | solution.py:23
  29.2 9.5 %broadcast_select_fusion = f32[40,8,23,256]{3,1,2,0:T(8,128)S(1)} fusion(pred[8,23]{0,1:T(8,128)(4,1)S(1)} %copy-done.9, bf16[3,3,256,256]{3,2,1,0:T(8,128)(2,1)S(1)} %copy-done, bf16[42,1,7,2,256]{4,2,3,0,1:T(8,128)(2,1)S(1)} %slice.36, bf16[42,1,8,23,256]{4,2,3,0,1:T(8,128)(2,1)S(1)} %copy.49), kind=kOutput, calls=%fused_computation.44 | convolution fusion | flops 8696995840 | bytes 12974264 | tf_op jit(solution)/shard_map/conv_general_dilated | solution.py:24
  38.8 2.6 %copy.50 = f32[40,8,23,256]{3,0,2,1:T(8,128)S(1)} copy(f32[40,8,23,256]{3,1,2,0:T(8,128)S(1)} %broadcast_select_fusion) | data formatting | bytes 15073280 | tf_op jit(solution)/shard_map/conv_general_dilated | solution.py:24
  41.4 4.2 %fusion.23 = f32[40,180,256]{2,0,1:T(8,128)} fusion(f32[40,1,184,256]{3,0,2,1:T(8,128)S(1)} %bitcast.42), kind=kLoop, calls=%fused_computation.33 | loop fusion | flops 14745600 | bytes 14745600 | tf_op jit(solution)/shard_map/mul | solution.py:57
  45.5 8.4 %reduce_window.7 = f32[20,90,256]{2,0,1:T(8,128)S(1)} reduce-window(f32[40,180,256]{2,0,1:T(8,128)} %fusion.23, f32[]{:T(128)} %constant.14.clone.1), window={size=2x2x1 stride=2x2x1}, to_apply=%region_0.0 | reduce-window | flops 1382400 | bytes 9216004 | tf_op jit(solution)/shard_map/reduce_window | solution.py:36
  57.8 33.8 %all-gather.2.cloned.1.call-done = bf16[20,720,128]{2,0,1:T(8,128)(2,1)} async-done(((bf16[20,90,128]{2,0,1:T(8,128)(2,1)}), bf16[20,720,128]{2,0,1:T(8,128)(2,1)}) %all-gather.2.cloned.1.call-update) | async-done | bytes 3686416 | tf_op jit(solution)/shard_map/all_gather | solution.py:63
  91.5 5.8 %copy_convert_fusion = f32[20,720,128]{2,1,0:T(8,128)} fusion(bf16[20,720,128]{2,0,1:T(8,128)(2,1)} %all-gather.2.cloned.1.call-done), kind=kLoop, calls=%fused_computation.45 | loop fusion | flops 1843200 | bytes 11059200 | tf_op jit(solution)/shard_map/convert_element_type | solution.py:47
  97.3 7.6 %add_convert_fusion = bf16[2,20,720,128]{3,2,1,0:T(8,128)(2,1)} fusion(f32[2,128]{1,0:T(2,128)S(1)} %fusion.36, f32[2,128]{1,0:T(2,128)S(1)} %convolution_add_fusion, f32[20,720,128]{2,1,0:T(8,128)} %copy_convert_fusion), kind=kLoop, calls=%fused_computation.13 | loop fusion | flops 11059200 | bytes 14747648 | tf_op jit(solution)/shard_map/convert_element_type | solution.py:48
  106.1 3.1 %collective-permute-start.4 = (bf16[2,1,720,128]{3,2,1,0:T(8,128)(2,1)S(1)}, bf16[2,1,720,128]{3,2,1,0:T(8,128)(2,1)S(1)}, u32[]{:S(2)}, u32[]{:S(2)}) collective-permute-start(bf16[2,1,720,128]{3,2,1,0:T(8,128)(2,1)S(1)} %get-tuple-element.5), channel_id=1, source_target_pairs={{0,8},{8,16},{16,24},{24,32},{32,40},{40,48},{48,56},{56,64},{64,7... | collective-permute-start | bytes 1105928 | tf_op jit(solution)/shard_map/ppermute | solution.py:16
  109.3 2.7 %collective-permute-start.5 = (bf16[2,1,720,128]{3,2,1,0:T(8,128)(2,1)S(1)}, bf16[2,1,720,128]{3,2,1,0:T(8,128)(2,1)S(1)}, u32[]{:S(2)}, u32[]{:S(2)}) collective-permute-start(bf16[2,1,720,128]{3,2,1,0:T(8,128)(2,1)S(1)} %get-tuple-element.6), channel_id=1, source_target_pairs={{8,0},{16,8},{24,16},{32,24},{40,32},{48,40},{56,48},{64,56},{72,6... | collective-permute-start | bytes 1105928 | tf_op jit(solution)/shard_map/ppermute | solution.py:17
  112.0 6.8 %collective-permute-done.4 = bf16[2,1,720,128]{3,2,1,0:T(8,128)(2,1)S(1)} collective-permute-done((bf16[2,1,720,128]{3,2,1,0:T(8,128)(2,1)S(1)}, bf16[2,1,720,128]{3,2,1,0:T(8,128)(2,1)S(1)}, u32[]{:S(2)}, u32[]{:S(2)}) %collective-permute-start.4) | collective-permute-done | bytes 368672 | tf_op jit(solution)/shard_map/ppermute | solution.py:16
  118.8 5.0 %collective-permute-done.5 = bf16[2,1,720,128]{3,2,1,0:T(8,128)(2,1)S(1)} collective-permute-done((bf16[2,1,720,128]{3,2,1,0:T(8,128)(2,1)S(1)}, bf16[2,1,720,128]{3,2,1,0:T(8,128)(2,1)S(1)}, u32[]{:S(2)}, u32[]{:S(2)}) %collective-permute-start.5) | collective-permute-done | bytes 368672 | tf_op jit(solution)/shard_map/ppermute | solution.py:17
  123.7 13.0 %fusion.15 = bf16[22,2,722,128]{3,2,0,1:T(8,128)(2,1)} fusion(bf16[2,1,720,128]{3,2,1,0:T(8,128)(2,1)S(1)} %collective-permute-done.5, bf16[2,20,720,128]{3,2,1,0:T(8,128)(2,1)} %add_convert_fusion, bf16[2,1,720,128]{3,2,1,0:T(8,128)(2,1)S(1)} %collective-permute-done.4), kind=kLoop, calls=%fused_computation.22 | loop fusion | flops 73193472 | bytes 16242688 | tf_op jit(solution)/shard_map/concatenate | solution.py:43
  136.8 7.0 %pad.2 = bf16[22,2,728,128]{3,2,0,1:T(8,128)(2,1)} pad(bf16[22,2,722,128]{3,2,0,1:T(8,128)(2,1)} %fusion.15, bf16[]{:T(256)} %constant.6), padding=0_0x0_0x0_6x0_0 | pad | bytes 16332802 | tf_op jit(solution)/shard_map/concatenate | solution.py:43
  143.8 12.6 %reshape.39 = bf16[22,2,8,91,128]{4,3,2,0,1:T(8,128)(2,1)} reshape(bf16[22,2,728,128]{3,2,0,1:T(8,128)(2,1)} %pad.2) | data formatting | bytes 16400384 | tf_op jit(solution)/shard_map/conv_general_dilated | solution.py:24
  157.7 4.6 %fusion.10 = bf16[22,2,8,93,128]{4,3,2,1,0:T(8,128)(2,1)S(1)} fusion(bf16[22,2,7,2,128]{4,3,2,1,0:T(2,128)(2,1)S(1)} %copy.77, bf16[22,2,8,91,128]{4,3,2,0,1:T(8,128)(2,1)} %reshape.39), kind=kLoop, calls=%fused_computation.15 | loop fusion | flops 25141248 | bytes 16738304 | tf_op jit(solution)/shard_map/conv_general_dilated | solution.py:24
  162.3 21.3 %fusion.8 = bf16[20,16,91,128]{3,1,2,0:T(8,128)(2,1)S(1)} fusion(bf16[3,3,128,128]{3,2,1,0:T(8,128)(2,1)S(1)} %copy-done.6, bf16[22,2,8,93,128]{4,3,2,1,0:T(8,128)(2,1)S(1)} %fusion.10, pred[16,91]{0,1:T(8,128)(4,1)S(1)} %copy-done.8), kind=kOutput, calls=%fused_computation.10 | convolution fusion | flops 8625111040 | bytes 16131504 | tf_op jit(solution)/shard_map/conv_general_dilated | solution.py:24
  183.6 5.1 %copy.56 = bf16[20,16,91,128]{3,2,1,0:T(8,128)(2,1)} copy(bf16[20,16,91,128]{3,1,2,0:T(8,128)(2,1)S(1)} %fusion.8) | data formatting | bytes 14909440 | tf_op jit(solution)/shard_map/convert_element_type | solution.py:79
  188.7 11.6 %reshape.27 = bf16[20,2,728,128]{3,2,1,0:T(8,128)(2,1)} reshape(bf16[20,16,91,128]{3,2,1,0:T(8,128)(2,1)} %copy.56) | data formatting | bytes 14909440 | tf_op jit(solution)/shard_map/convert_element_type | solution.py:79
  200.3 12.3 %fusion.9 = bf16[2,20,720,128]{3,2,1,0:T(8,128)(2,1)} fusion(bf16[2,20,720,128]{3,2,1,0:T(8,128)(2,1)} %add_convert_fusion, bf16[720,720]{1,0:T(8,128)(2,1)S(1)} %copy-done.5, bf16[20,2,728,128]{3,2,1,0:T(8,128)(2,1)} %reshape.27), kind=kOutput, calls=%fused_computation.12 | convolution fusion | flops 5319475200 | bytes 23155200 | tf_op jit(solution)/shard_map/ij,bajc->baic/dot_general | solution.py:80
  (47 shorter events, 12.8 us)
Async XLA Ops:
  6.5 22.7 %copy-start = (bf16[3,3,256,256]{3,2,1,0:T(8,128)(2,1)S(1)}, bf16[3,3,256,256]{3,2,1,0:T(8,128)(2,1)}, u32[]{:S(2)}) copy-start(bf16[3,3,256,256]{3,2,1,0:T(8,128)(2,1)} %param.9) | copy-start | bytes 3538948
  6.5 85.0 %all-gather.2.cloned.1.call-start = ((), (), s32[]{:S(2)}) async-start(), calls=%async_computation | async-start | bytes 4976640 | tf_op jit(solution)/shard_map/all_gather | solution.py:63
  6.5 17.5 %copy-start.2 = (bf16[40,180,256]{2,0,1:T(8,128)(2,1)S(1)}, bf16[40,180,256]{2,0,1:T(8,128)(2,1)}, u32[]{:S(2)}) copy-start(bf16[40,180,256]{2,0,1:T(8,128)(2,1)} %param.8) | copy-start | bytes 11059204
  8.4 8.7 %collective-permute-start.1 = (bf16[1,180,256]{2,1,0:T(8,128)(2,1)S(1)}, bf16[1,180,256]{2,1,0:T(8,128)(2,1)S(1)}, u32[]{:S(2)}, u32[]{:S(2)}) collective-permute-start(bf16[1,180,256]{2,1,0:T(8,128)(2,1)S(1)} %copy.64), channel_id=1, source_target_pairs={{8,0},{16,8},{24,16},{32,24},{40,32},{48,40},{56,48},{64,56},{72,6... | collective-permute-start | bytes 276488 | tf_op jit(solution)/shard_map/ppermute | solution.py:17
  10.8 7.8 %collective-permute-start = (bf16[1,180,256]{2,1,0:T(8,128)(2,1)S(1)}, bf16[1,180,256]{2,1,0:T(8,128)(2,1)S(1)}, u32[]{:S(2)}, u32[]{:S(2)}) collective-permute-start(bf16[1,180,256]{2,1,0:T(8,128)(2,1)S(1)} %copy.63), channel_id=1, source_target_pairs={{0,8},{8,16},{16,24},{24,32},{32,40},{40,48},{48,56},{56,64},{64,7... | collective-permute-start | bytes 276488 | tf_op jit(solution)/shard_map/ppermute | solution.py:16
  19.5 4.5 %collective-permute-start.2 = (bf16[42,1,256]{2,0,1:T(8,128)(2,1)S(1)}, bf16[42,1,256]{2,0,1:T(8,128)(2,1)S(1)}, u32[]{:S(2)}, u32[]{:S(2)}) collective-permute-start(bf16[42,1,256]{2,0,1:T(8,128)(2,1)S(1)} %get-tuple-element.7), channel_id=1, source_target_pairs={{0,1},{1,2},{2,3},{3,4},{4,5},{5,6},{6,7},{7,0},{8,9},{9,10},{10,1... | collective-permute-start | bytes 64520 | tf_op jit(solution)/shard_map/ppermute | solution.py:16
  19.6 4.5 %collective-permute-start.3 = (bf16[42,1,256]{2,0,1:T(8,128)(2,1)S(1)}, bf16[42,1,256]{2,0,1:T(8,128)(2,1)S(1)}, u32[]{:S(2)}, u32[]{:S(2)}) collective-permute-start(bf16[42,1,256]{2,0,1:T(8,128)(2,1)S(1)} %get-tuple-element.8), channel_id=1, source_target_pairs={{1,0},{2,1},{3,2},{4,3},{5,4},{6,5},{7,6},{0,7},{9,8},{10,9},{11,1... | collective-permute-start | bytes 64520 | tf_op jit(solution)/shard_map/ppermute | solution.py:17
  27.2 2.0 copy-start.9
  45.5 9.1 %copy-start.4 = (bf16[256,128]{1,0:T(8,128)(2,1)S(1)}, bf16[256,128]{1,0:T(8,128)(2,1)}, u32[]{:S(2)}) copy-start(bf16[256,128]{1,0:T(8,128)(2,1)} %param.10) | copy-start | bytes 196612
  45.5 10.7 %copy-start.7 = (s32[16]{0:T(128)S(1)}, s32[16]{0:T(128)}, u32[]{:S(2)}) copy-start(s32[16]{0:T(128)} %param.13) | copy-start | bytes 196
  54.1 3.4 %copy-start.3 = (f32[720,128]{1,0:T(8,128)S(1)}, f32[720,128]{1,0:T(8,128)}, u32[]{:S(2)}) copy-start(f32[720,128]{1,0:T(8,128)} %param.12) | copy-start | bytes 1105924
  106.1 12.6 %collective-permute-start.4 = (bf16[2,1,720,128]{3,2,1,0:T(8,128)(2,1)S(1)}, bf16[2,1,720,128]{3,2,1,0:T(8,128)(2,1)S(1)}, u32[]{:S(2)}, u32[]{:S(2)}) collective-permute-start(bf16[2,1,720,128]{3,2,1,0:T(8,128)(2,1)S(1)} %get-tuple-element.5), channel_id=1, source_target_pairs={{0,8},{8,16},{16,24},{24,32},{32,40},{40,48},{48,56},{56,64},{64,7... | collective-permute-start | bytes 1105928 | tf_op jit(solution)/shard_map/ppermute | solution.py:16
  109.3 14.5 %collective-permute-start.5 = (bf16[2,1,720,128]{3,2,1,0:T(8,128)(2,1)S(1)}, bf16[2,1,720,128]{3,2,1,0:T(8,128)(2,1)S(1)}, u32[]{:S(2)}, u32[]{:S(2)}) collective-permute-start(bf16[2,1,720,128]{3,2,1,0:T(8,128)(2,1)S(1)} %get-tuple-element.6), channel_id=1, source_target_pairs={{8,0},{16,8},{24,16},{32,24},{40,32},{48,40},{56,48},{64,56},{72,6... | collective-permute-start | bytes 1105928 | tf_op jit(solution)/shard_map/ppermute | solution.py:17
  157.7 4.6 %copy-start.6 = (bf16[3,3,128,128]{3,2,1,0:T(8,128)(2,1)S(1)}, bf16[3,3,128,128]{3,2,1,0:T(8,128)(2,1)}, u32[]{:S(2)}) copy-start(bf16[3,3,128,128]{3,2,1,0:T(8,128)(2,1)} %param.14) | copy-start | bytes 884740
  157.7 4.6 %copy-start.8 = (pred[16,91]{0,1:T(8,128)(4,1)S(1)}, pred[16,91]{0,1:T(8,128)(4,1)}, u32[]{:S(2)}) copy-start(pred[16,91]{0,1:T(8,128)(4,1)} %constant.37) | copy-start | bytes 4372
  188.7 11.6 %copy-start.5 = (bf16[720,720]{1,0:T(8,128)(2,1)S(1)}, bf16[720,720]{1,0:T(8,128)(2,1)}, u32[]{:S(2)}) copy-start(bf16[720,720]{1,0:T(8,128)(2,1)} %param.15) | copy-start | bytes 3110404
  200.3 12.3 %copy-start.1 = (bf16[3,3,256,256]{3,2,1,0:T(8,128)(2,1)S(1)}, bf16[3,3,256,256]{3,2,1,0:T(8,128)(2,1)}, u32[]{:S(2)}) copy-start(bf16[3,3,256,256]{3,2,1,0:T(8,128)(2,1)} %param.9) | copy-start | bytes 3538948
Sparse Core Ops, SparseCore 0:
  56.3 35.2 all-gather.1
where the time goes:
time: 223 us; the launch traced here: 220 us
  waiting for transfers between devices  49.1 us (22%)
  other arithmetic  47.8 us (21%)
  local copies, waits for them, and re-layouts  47 us (21%)
  matrix products  45 us (20%)
  starting transfers between devices  16.9 us (8%)
  between operations  13.9 us (6%)
    all_gather x1, waiting for transfers between devices, shards(): lax.all_gather(flat.astype(jnp.bfloat16).reshape(pooled.shape[0], pooled....  33.8 us
    conv_general_dilated x2, matrix products, conv_three(): lax.conv_general_dilated(batched, weight, (1, 1), 'VALID', dimension_numb...  30.8 us
    conv_general_dilated x5, local copies, waits for them, and re-layouts, conv_three(): lax.conv_general_dilated(batched, weight, (1, 1), 'VALID', dimension_numb...  17.9 us
    convert_element_type x2, local copies, waits for them, and re-layouts, shards(): hidden = jax.nn.gelu(conv_three(padded_head, w_head)).astype(jnp.bfloat16)  16.7 us
    concatenate x1, other arithmetic, wrap_columns(): jnp.concatenate([field[..., -1:, :], field, field[..., :1, :]], axis=-2)  13 us
    dot_general x1, matrix products, shards(): jnp.einsum('ij,bajc->baic', zonal_mix, hidden, preferred_element_type=jnp...  12.3 us
    ppermute x3, waiting for transfers between devices, extended(): before = lax.ppermute(last, axis, up)  9.7 us
    ppermute x3, starting transfers between devices, extended(): before = lax.ppermute(last, axis, up)  8.78 us
  transfers between devices with their start and end apart: 7, of which 6 were waited for; matrix products, arithmetic and copies ran while one was open for 1% of the time, Pallas kernels for 0%

commit v1 on v0

--- a/solution.py
+++ b/solution.py
@@ -2,6 +2,7 @@
 import jax.numpy as jnp
 from jax import lax
 from jax.sharding import PartitionSpec as P
+from jax.lax import all_to_all, axis_size
 
 LEAD_DEV = 2
 
@@ -60,11 +61,16 @@
     lon_group = lax.axis_index("lon")
     my_rows = lax.dynamic_slice_in_dim(lead_ids, lon_group * LEAD_DEV, LEAD_DEV)
     flat = jnp.dot(pooled.reshape(-1, channels), w_proj, preferred_element_type=jnp.float32)
-    band_proj = lax.all_gather(
-        flat.astype(jnp.bfloat16).reshape(pooled.shape[0], pooled.shape[1], head_width),
-        "lon",
-        axis=1,
-        tiled=True,
+
+    def hold_words(body, shard_axis):
+        main = axis_size(shard_axis)
+        step_out = jnp.stack(main * [body], axis=0)
+        outcome_arr = all_to_all(step_out, shard_axis, 0, 0)
+        left_arr = jnp.concatenate(outcome_arr, axis=1)
+        return left_arr
+
+    band_proj = hold_words(
+        flat.astype(jnp.bfloat16).reshape(pooled.shape[0], pooled.shape[1], head_width), "lon"
     )
     onehot = (my_rows[:, None] == jnp.arange(film_scale.shape[0], dtype=jnp.int32)[None, :]).astype(
         jnp.float32

time: 223 us -> 240 us (1.076)
  local copies, waits for them, and re-layouts: 47 us -> 61.1 us
  between operations: 13.9 us -> 0.58 us
  waiting for transfers between devices: 49.1 us -> 61.7 us
  starting transfers between devices: 16.9 us -> 23.9 us
  other arithmetic: 47.8 us -> 45.2 us
    all_to_all x0 -> x1, waiting for transfers between devices: none -> 46.2 us  [hold_words(): outcome_arr = all_to_all(step_out, shard_axis, 0, 0)]
    all_gather x1 -> x0, waiting for transfers between devices: 33.8 us -> none  [shards(): lax.all_gather(flat.astype(jnp.bfloat16).reshape(pooled.shape[0], pooled....]
    convert_element_type x0 -> x2, local copies, waits for them, and re-layouts: none -> 12.5 us  [modulate(): widened = projected.astype(jnp.float32)[None]]
    all_to_all x0 -> x1, starting transfers between devices: none -> 4.52 us  [hold_words(): outcome_arr = all_to_all(step_out, shard_axis, 0, 0)]
    ppermute x3, starting transfers between devices: 8.78 us -> 12.1 us  [extended(): before = lax.ppermute(last, axis, up)]
    another operation x0 -> x2, local copies, waits for them, and re-layouts: none -> 2.71 us  [hold_words(): step_out = jnp.stack(main * [body], axis=0)]
    convert_element_type x1, other arithmetic: 5.79 us -> 3.19 us  [modulate(): widened = projected.astype(jnp.float32)[None]]
  transfers between devices with their start and end apart: 7 -> 7, of which waited for: 6 -> 6; matrix products, arithmetic and copies ran while one was open for 1% -> 0% of each run, Pallas kernels for 0% -> 0%
where the time goes in v1:
time: 240 us; the launch traced here: 236 us
  waiting for transfers between devices  61.7 us (26%)
  local copies, waits for them, and re-layouts  61.1 us (25%)
  other arithmetic  45.2 us (19%)
  matrix products  44 us (18%)
  starting transfers between devices  23.9 us (10%)
    all_to_all x1, waiting for transfers between devices, hold_words(): outcome_arr = all_to_all(step_out, shard_axis, 0, 0)  46.2 us
    conv_general_dilated x2, matrix products, conv_three(): lax.conv_general_dilated(batched, weight, (1, 1), 'VALID', dimension_numb...  30.8 us
    conv_general_dilated x5, local copies, waits for them, and re-layouts, conv_three(): lax.conv_general_dilated(batched, weight, (1, 1), 'VALID', dimension_numb...  17.9 us
    convert_element_type x2, local copies, waits for them, and re-layouts, shards(): hidden = jax.nn.gelu(conv_three(padded_head, w_head)).astype(jnp.bfloat16)  16.7 us
    concatenate x1, other arithmetic, wrap_columns(): jnp.concatenate([field[..., -1:, :], field, field[..., :1, :]], axis=-2)  13 us
    convert_element_type x2, local copies, waits for them, and re-layouts, modulate(): widened = projected.astype(jnp.float32)[None]  12.5 us
    dot_general x1, matrix products, shards(): jnp.einsum('ij,bajc->baic', zonal_mix, hidden, preferred_element_type=jnp...  12.3 us
    ppermute x3, starting transfers between devices, extended(): before = lax.ppermute(last, axis, up)  12.1 us
  transfers between devices with their start and end apart: 7, of which 6 were waited for; matrix products, arithmetic and copies ran while one was open for 0% of the time, Pallas kernels for 0%

profile of v1, /device:TPU:96, one launch (start us, length us, event | category | flops | bytes accessed | tf_op | source)
XLA Modules:
  0.0 236.5 jit_solution(2399598342748320848)
XLA Ops:
  4.3 5.6 %collective-permute-start = (bf16[1,180,256]{2,1,0:T(8,128)(2,1)S(1)}, bf16[1,180,256]{2,1,0:T(8,128)(2,1)S(1)}, u32[]{:S(2)}, u32[]{:S(2)}) collective-permute-start(bf16[1,180,256]{2,1,0:T(8,128)(2,1)S(1)} %copy.47), channel_id=1, source_target_pairs={{0,8},{8,16},{16,24},{24,32},{32,40},{40,48},{48,56},{56,64},{64,7... | collective-permute-start | bytes 276488 | tf_op jit(solution)/shard_map/ppermute | solution.py:17
  13.0 2.9 %collective-permute-start.3 = (bf16[42,1,256]{2,0,1:T(8,128)(2,1)S(1)}, bf16[42,1,256]{2,0,1:T(8,128)(2,1)S(1)}, u32[]{:S(2)}, u32[]{:S(2)}) collective-permute-start(bf16[42,1,256]{2,0,1:T(8,128)(2,1)S(1)} %get-tuple-element.8), channel_id=1, source_target_pairs={{1,0},{2,1},{3,2},{4,3},{5,4},{6,5},{7,6},{0,7},{9,8},{10,9},{11,1... | collective-permute-start | bytes 64520 | tf_op jit(solution)/shard_map/ppermute | solution.py:18
  17.5 3.2 %maximum_bitcast_fusion = bf16[42,1,182,256]{3,0,2,1:T(8,128)(2,1)S(1)} fusion(bf16[42,1,256]{2,0,1:T(8,128)(2,1)S(1)} %collective-permute-done.3, bf16[1,180,256]{2,0,1:T(2,128)(2,1)S(1)} %copy.31, bf16[40,180,256]{2,0,1:T(8,128)(2,1)S(1)} %copy-done.2, bf16[1,180,256]{2,0,1:T(2,128)(2,1)S(1)} %copy.30, bf16[42,1,256]{2,0,1:T(8,128)(2,1)S(1)} %collective-permute-done.2), kind=kLoop, calls=%fused_computation.38 | loop fusion | flops 19568640 | bytes 7827456 | tf_op jit(solution)/shard_map/broadcast_in_dim | solution.py:24
  22.7 9.5 %broadcast_select_fusion = f32[40,8,23,256]{3,1,2,0:T(8,128)S(1)} fusion(pred[8,23]{0,1:T(8,128)(4,1)S(1)} %copy-done.10, bf16[3,3,256,256]{3,2,1,0:T(8,128)(2,1)S(1)} %copy-done, bf16[42,1,7,2,256]{4,2,3,0,1:T(8,128)(2,1)S(1)} %slice.36, bf16[42,1,8,23,256]{4,2,3,0,1:T(8,128)(2,1)S(1)} %copy.34), kind=kOutput, calls=%fused_computation.45 | convolution fusion | flops 8696995840 | bytes 12974264 | tf_op jit(solution)/shard_map/conv_general_dilated | solution.py:25
  32.2 2.6 %copy.35 = f32[40,8,23,256]{3,0,2,1:T(8,128)S(1)} copy(f32[40,8,23,256]{3,1,2,0:T(8,128)S(1)} %broadcast_select_fusion) | data formatting | bytes 15073280 | tf_op jit(solution)/shard_map/conv_general_dilated | solution.py:25
  34.8 4.2 %fusion.23 = f32[40,180,256]{2,0,1:T(8,128)} fusion(f32[40,1,184,256]{3,0,2,1:T(8,128)S(1)} %bitcast.44), kind=kLoop, calls=%fused_computation.34 | loop fusion | flops 14745600 | bytes 14745600 | tf_op jit(solution)/shard_map/mul | solution.py:58
  39.0 8.4 %reduce_window.7 = f32[20,90,256]{2,0,1:T(8,128)S(1)} reduce-window(f32[40,180,256]{2,0,1:T(8,128)} %fusion.23, f32[]{:T(128)} %constant.14.clone.1), window={size=2x2x1 stride=2x2x1}, to_apply=%region_0.0 | reduce-window | flops 1382400 | bytes 9216004 | tf_op jit(solution)/shard_map/reduce_window | solution.py:37
  51.2 4.5 %all-to-all-start = ((bf16[8,20,90,128]{3,2,1,0:T(8,128)(2,1)}), bf16[8,20,90,128]{3,2,1,0:T(8,128)(2,1)}, u32[]{:S(2)}, u32[]{:S(2)}) async-start(bf16[8,20,90,128]{3,2,1,0:T(8,128)(2,1)} %stack.3), calls=%async_computation | async-start | bytes 7864320 | tf_op jit(solution)/shard_map/all_to_all | solution.py:68
  56.4 46.2 %all-to-all-done = bf16[8,20,90,128]{3,2,1,0:T(8,128)(2,1)} async-done(((bf16[8,20,90,128]{3,2,1,0:T(8,128)(2,1)}), bf16[8,20,90,128]{3,2,1,0:T(8,128)(2,1)}, u32[]{:S(2)}, u32[]{:S(2)}) %all-to-all-start) | async-done | bytes 3686432 | tf_op jit(solution)/shard_map/all_to_all | solution.py:68
  102.6 3.2 %convert_bitcast_fusion = f32[20,8,90,128]{3,2,0,1:T(8,128)S(1)} fusion(bf16[8,20,90,128]{3,2,1,0:T(8,128)(2,1)} %all-to-all-done), kind=kLoop, calls=%fused_computation.27 | loop fusion | flops 1843200 | bytes 11059200 | tf_op jit(solution)/shard_map/convert_element_type | solution.py:48
  105.8 4.0 %copy.37 = f32[20,8,90,128]{3,2,1,0:T(8,128)} copy(f32[20,8,90,128]{3,2,0,1:T(8,128)S(1)} %convert_bitcast_fusion) | data formatting | bytes 14745600 | tf_op jit(solution)/shard_map/convert_element_type | solution.py:48
  109.8 8.5 %reshape.34 = f32[20,720,128]{2,1,0:T(8,128)} reshape(f32[20,8,90,128]{3,2,1,0:T(8,128)} %copy.37) | data formatting | bytes 14745600 | tf_op jit(solution)/shard_map/convert_element_type | solution.py:48
  118.3 7.6 %add_convert_fusion = bf16[2,20,720,128]{3,2,1,0:T(8,128)(2,1)} fusion(f32[2,128]{1,0:T(2,128)S(1)} %fusion.36, f32[2,128]{1,0:T(2,128)S(1)} %convolution_add_fusion, f32[20,720,128]{2,1,0:T(8,128)} %reshape.34), kind=kLoop, calls=%fused_computation.13 | loop fusion | flops 11059200 | bytes 14747648 | tf_op jit(solution)/shard_map/convert_element_type | solution.py:49
  127.1 6.4 %collective-permute-start.4 = (bf16[2,1,720,128]{3,2,1,0:T(8,128)(2,1)S(1)}, bf16[2,1,720,128]{3,2,1,0:T(8,128)(2,1)S(1)}, u32[]{:S(2)}, u32[]{:S(2)}) collective-permute-start(bf16[2,1,720,128]{3,2,1,0:T(8,128)(2,1)S(1)} %get-tuple-element.5), channel_id=1, source_target_pairs={{0,8},{8,16},{16,24},{24,32},{32,40},{40,48},{48,56},{56,64},{64,7... | collective-permute-start | bytes 1105928 | tf_op jit(solution)/shard_map/ppermute | solution.py:17
  135.4 5.7 %collective-permute-done.4 = bf16[2,1,720,128]{3,2,1,0:T(8,128)(2,1)S(1)} collective-permute-done((bf16[2,1,720,128]{3,2,1,0:T(8,128)(2,1)S(1)}, bf16[2,1,720,128]{3,2,1,0:T(8,128)(2,1)S(1)}, u32[]{:S(2)}, u32[]{:S(2)}) %collective-permute-start.4) | collective-permute-done | bytes 368672 | tf_op jit(solution)/shard_map/ppermute | solution.py:17
  141.1 6.2 %collective-permute-done.5 = bf16[2,1,720,128]{3,2,1,0:T(8,128)(2,1)S(1)} collective-permute-done((bf16[2,1,720,128]{3,2,1,0:T(8,128)(2,1)S(1)}, bf16[2,1,720,128]{3,2,1,0:T(8,128)(2,1)S(1)}, u32[]{:S(2)}, u32[]{:S(2)}) %collective-permute-start.5) | collective-permute-done | bytes 368672 | tf_op jit(solution)/shard_map/ppermute | solution.py:18
  147.4 13.0 %fusion.15 = bf16[22,2,722,128]{3,2,0,1:T(8,128)(2,1)} fusion(bf16[2,1,720,128]{3,2,1,0:T(8,128)(2,1)S(1)} %collective-permute-done.5, bf16[2,20,720,128]{3,2,1,0:T(8,128)(2,1)} %add_convert_fusion, bf16[2,1,720,128]{3,2,1,0:T(8,128)(2,1)S(1)} %collective-permute-done.4), kind=kLoop, calls=%fused_computation.22 | loop fusion | flops 73193472 | bytes 16242688 | tf_op jit(solution)/shard_map/concatenate | solution.py:44
  160.4 7.0 %pad.2 = bf16[22,2,728,128]{3,2,0,1:T(8,128)(2,1)} pad(bf16[22,2,722,128]{3,2,0,1:T(8,128)(2,1)} %fusion.15, bf16[]{:T(256)} %constant.6), padding=0_0x0_0x0_6x0_0 | pad | bytes 16332802 | tf_op jit(solution)/shard_map/concatenate | solution.py:44
  167.4 12.6 %reshape.46 = bf16[22,2,8,91,128]{4,3,2,0,1:T(8,128)(2,1)} reshape(bf16[22,2,728,128]{3,2,0,1:T(8,128)(2,1)} %pad.2) | data formatting | bytes 16400384 | tf_op jit(solution)/shard_map/conv_general_dilated | solution.py:25
  181.3 4.6 %fusion.10 = bf16[22,2,8,93,128]{4,3,2,1,0:T(8,128)(2,1)S(1)} fusion(bf16[22,2,7,2,128]{4,3,2,1,0:T(2,128)(2,1)S(1)} %copy.60, bf16[22,2,8,91,128]{4,3,2,0,1:T(8,128)(2,1)} %reshape.46), kind=kLoop, calls=%fused_computation.15 | loop fusion | flops 25141248 | bytes 16738304 | tf_op jit(solution)/shard_map/conv_general_dilated | solution.py:25
  186.0 21.3 %fusion.8 = bf16[20,16,91,128]{3,1,2,0:T(8,128)(2,1)S(1)} fusion(bf16[3,3,128,128]{3,2,1,0:T(8,128)(2,1)S(1)} %copy-done.7, bf16[22,2,8,93,128]{4,3,2,1,0:T(8,128)(2,1)S(1)} %fusion.10, pred[16,91]{0,1:T(8,128)(4,1)S(1)} %copy-done.9), kind=kOutput, calls=%fused_computation.10 | convolution fusion | flops 8625111040 | bytes 16131504 | tf_op jit(solution)/shard_map/conv_general_dilated | solution.py:25
  207.3 5.1 %copy.40 = bf16[20,16,91,128]{3,2,1,0:T(8,128)(2,1)} copy(bf16[20,16,91,128]{3,1,2,0:T(8,128)(2,1)S(1)} %fusion.8) | data formatting | bytes 14909440 | tf_op jit(solution)/shard_map/convert_element_type | solution.py:85
  212.4 11.6 %reshape.33 = bf16[20,2,728,128]{3,2,1,0:T(8,128)(2,1)} reshape(bf16[20,16,91,128]{3,2,1,0:T(8,128)(2,1)} %copy.40) | data formatting | bytes 14909440 | tf_op jit(solution)/shard_map/convert_element_type | solution.py:85
  223.9 12.3 %fusion.9 = bf16[2,20,720,128]{3,2,1,0:T(8,128)(2,1)} fusion(bf16[2,20,720,128]{3,2,1,0:T(8,128)(2,1)} %add_convert_fusion, bf16[720,720]{1,0:T(8,128)(2,1)S(1)} %copy-done.6, bf16[20,2,728,128]{3,2,1,0:T(8,128)(2,1)} %reshape.33), kind=kOutput, calls=%fused_computation.12 | convolution fusion | flops 5319475200 | bytes 23155200 | tf_op jit(solution)/shard_map/ij,bajc->baic/dot_general | solution.py:86
  (50 shorter events, 19.6 us)
Async XLA Ops:
  0.0 22.7 %copy-start = (bf16[3,3,256,256]{3,2,1,0:T(8,128)(2,1)S(1)}, bf16[3,3,256,256]{3,2,1,0:T(8,128)(2,1)}, u32[]{:S(2)}) copy-start(bf16[3,3,256,256]{3,2,1,0:T(8,128)(2,1)} %param.9) | copy-start | bytes 3538948
  0.0 17.5 %copy-start.2 = (bf16[40,180,256]{2,0,1:T(8,128)(2,1)S(1)}, bf16[40,180,256]{2,0,1:T(8,128)(2,1)}, u32[]{:S(2)}) copy-start(bf16[40,180,256]{2,0,1:T(8,128)(2,1)} %param.8) | copy-start | bytes 11059204
  1.8 8.7 %collective-permute-start.1 = (bf16[1,180,256]{2,1,0:T(8,128)(2,1)S(1)}, bf16[1,180,256]{2,1,0:T(8,128)(2,1)S(1)}, u32[]{:S(2)}, u32[]{:S(2)}) collective-permute-start(bf16[1,180,256]{2,1,0:T(8,128)(2,1)S(1)} %copy.48), channel_id=1, source_target_pairs={{8,0},{16,8},{24,16},{32,24},{40,32},{48,40},{56,48},{64,56},{72,6... | collective-permute-start | bytes 276488 | tf_op jit(solution)/shard_map/ppermute | solution.py:18
  4.3 7.8 %collective-permute-start = (bf16[1,180,256]{2,1,0:T(8,128)(2,1)S(1)}, bf16[1,180,256]{2,1,0:T(8,128)(2,1)S(1)}, u32[]{:S(2)}, u32[]{:S(2)}) collective-permute-start(bf16[1,180,256]{2,1,0:T(8,128)(2,1)S(1)} %copy.47), channel_id=1, source_target_pairs={{0,8},{8,16},{16,24},{24,32},{32,40},{40,48},{48,56},{56,64},{64,7... | collective-permute-start | bytes 276488 | tf_op jit(solution)/shard_map/ppermute | solution.py:17
  13.0 4.5 %collective-permute-start.2 = (bf16[42,1,256]{2,0,1:T(8,128)(2,1)S(1)}, bf16[42,1,256]{2,0,1:T(8,128)(2,1)S(1)}, u32[]{:S(2)}, u32[]{:S(2)}) collective-permute-start(bf16[42,1,256]{2,0,1:T(8,128)(2,1)S(1)} %get-tuple-element.7), channel_id=1, source_target_pairs={{0,1},{1,2},{2,3},{3,4},{4,5},{5,6},{6,7},{7,0},{8,9},{9,10},{10,1... | collective-permute-start | bytes 64520 | tf_op jit(solution)/shard_map/ppermute | solution.py:17
  13.0 4.5 %collective-permute-start.3 = (bf16[42,1,256]{2,0,1:T(8,128)(2,1)S(1)}, bf16[42,1,256]{2,0,1:T(8,128)(2,1)S(1)}, u32[]{:S(2)}, u32[]{:S(2)}) collective-permute-start(bf16[42,1,256]{2,0,1:T(8,128)(2,1)S(1)} %get-tuple-element.8), channel_id=1, source_target_pairs={{1,0},{2,1},{3,2},{4,3},{5,4},{6,5},{7,6},{0,7},{9,8},{10,9},{11,1... | collective-permute-start | bytes 64520 | tf_op jit(solution)/shard_map/ppermute | solution.py:18
  20.7 2.0 copy-start.10
  39.0 9.1 %copy-start.5 = (bf16[256,128]{1,0:T(8,128)(2,1)S(1)}, bf16[256,128]{1,0:T(8,128)(2,1)}, u32[]{:S(2)}) copy-start(bf16[256,128]{1,0:T(8,128)(2,1)} %param.10) | copy-start | bytes 196612
  47.8 8.0 %copy-start.8 = (s32[16]{0:T(128)S(1)}, s32[16]{0:T(128)}, u32[]{:S(2)}) copy-start(s32[16]{0:T(128)} %param.13) | copy-start | bytes 196
  47.8 8.0 %copy-start.3 = (f32[720,128]{1,0:T(8,128)S(1)}, f32[720,128]{1,0:T(8,128)}, u32[]{:S(2)}) copy-start(f32[720,128]{1,0:T(8,128)} %param.11) | copy-start | bytes 1105924
  47.8 8.3 %copy-start.4 = (f32[720,128]{1,0:T(8,128)S(1)}, f32[720,128]{1,0:T(8,128)}, u32[]{:S(2)}) copy-start(f32[720,128]{1,0:T(8,128)} %param.12) | copy-start | bytes 1105924
  51.2 51.4 %all-to-all-start = ((bf16[8,20,90,128]{3,2,1,0:T(8,128)(2,1)}), bf16[8,20,90,128]{3,2,1,0:T(8,128)(2,1)}, u32[]{:S(2)}, u32[]{:S(2)}) async-start(bf16[8,20,90,128]{3,2,1,0:T(8,128)(2,1)} %stack.3), calls=%async_computation | async-start | bytes 7864320 | tf_op jit(solution)/shard_map/all_to_all | solution.py:68
  127.1 14.0 %collective-permute-start.4 = (bf16[2,1,720,128]{3,2,1,0:T(8,128)(2,1)S(1)}, bf16[2,1,720,128]{3,2,1,0:T(8,128)(2,1)S(1)}, u32[]{:S(2)}, u32[]{:S(2)}) collective-permute-start(bf16[2,1,720,128]{3,2,1,0:T(8,128)(2,1)S(1)} %get-tuple-element.5), channel_id=1, source_target_pairs={{0,8},{8,16},{16,24},{24,32},{32,40},{40,48},{48,56},{56,64},{64,7... | collective-permute-start | bytes 1105928 | tf_op jit(solution)/shard_map/ppermute | solution.py:17
  133.5 13.9 %collective-permute-start.5 = (bf16[2,1,720,128]{3,2,1,0:T(8,128)(2,1)S(1)}, bf16[2,1,720,128]{3,2,1,0:T(8,128)(2,1)S(1)}, u32[]{:S(2)}, u32[]{:S(2)}) collective-permute-start(bf16[2,1,720,128]{3,2,1,0:T(8,128)(2,1)S(1)} %get-tuple-element.6), channel_id=1, source_target_pairs={{8,0},{16,8},{24,16},{32,24},{40,32},{48,40},{56,48},{64,56},{72,6... | collective-permute-start | bytes 1105928 | tf_op jit(solution)/shard_map/ppermute | solution.py:18
  181.3 4.6 %copy-start.7 = (bf16[3,3,128,128]{3,2,1,0:T(8,128)(2,1)S(1)}, bf16[3,3,128,128]{3,2,1,0:T(8,128)(2,1)}, u32[]{:S(2)}) copy-start(bf16[3,3,128,128]{3,2,1,0:T(8,128)(2,1)} %param.14) | copy-start | bytes 884740
  181.3 4.6 %copy-start.9 = (pred[16,91]{0,1:T(8,128)(4,1)S(1)}, pred[16,91]{0,1:T(8,128)(4,1)}, u32[]{:S(2)}) copy-start(pred[16,91]{0,1:T(8,128)(4,1)} %constant.37) | copy-start | bytes 4372
  212.4 11.6 %copy-start.6 = (bf16[720,720]{1,0:T(8,128)(2,1)S(1)}, bf16[720,720]{1,0:T(8,128)(2,1)}, u32[]{:S(2)}) copy-start(bf16[720,720]{1,0:T(8,128)(2,1)} %param.15) | copy-start | bytes 3110404
  223.9 12.3 %copy-start.1 = (bf16[3,3,256,256]{3,2,1,0:T(8,128)(2,1)S(1)}, bf16[3,3,256,256]{3,2,1,0:T(8,128)(2,1)}, u32[]{:S(2)}) copy-start(bf16[3,3,256,256]{3,2,1,0:T(8,128)(2,1)} %param.9) | copy-start | bytes 3538948
